TPU v7x, 32 devices: a whole 2x2x4 slice. The times are simulated.
32 devices in a mesh: dp: 16 (over z, y, x), seq: 2 (over core).
Axes of the slice: x: 2, y: 2, z: 4, core: 2. Of those that a mesh axis runs over, the one named last changes fastest.
Arguments:
- tokens: bfloat16 [16, 2048, 1120], P('dp', 'seq'), may hold values from -6 to 6
- cotangent: bfloat16 [16, 2048, 1120], P('dp', 'seq'), may hold values from -6 to 6
- pad_mask: int32 [16, 2048], P('dp', 'seq'), may hold values from 0 to 1, as said below
- prefix_len: int32 [16], P('dp'), may hold values from 1 to 128
- norm_gains: float32 [2, 1120], replicated, may hold values from 0.5 to 1.5
- norm_shifts: float32 [2, 1120], replicated, may hold values from -1.8 to 1.8
- owner_map: int32 [192], replicated, may hold values from 0 to 191, as said below
- weight_copy: bfloat16 [192, 280, 280], P('dp'), may hold values from -1.8090681 to 1.8090681
- master: float32 [192, 280, 280], P('dp'), may hold values from -1.8090681 to 1.8090681
- average_weights: float32 [192, 280, 280], P('dp'), may hold values from -1.8090681 to 1.8090681
- stat_left: float32 [192, 280, 280], P('dp'), may hold values from -16.290909 to 36.654545, as said below
- stat_right: float32 [192, 280, 280], P('dp'), may hold values from -16.290909 to 36.654545, as said below
- root_left: float32 [192, 280, 280], P('dp'), may hold values from -3 to 5, as said below
- root_right: float32 [192, 280, 280], P('dp'), may hold values from -3 to 5, as said below
Outputs:
- block_out: bfloat16 [16, 2048, 1120], P('dp', 'seq')
- grad_input: float32 [16, 2048, 1120], P('dp', 'seq')
- norm_grad: float32 [4, 1120], replicated
- new_norms: float32 [4, 1120], replicated
- slot_grad: float32 [192, 280, 280], P('dp')
- new_left: float32 [192, 280, 280], P('dp')
- new_right: float32 [192, 280, 280], P('dp')
- new_master: float32 [192, 280, 280], P('dp')
- new_copy: bfloat16 [192, 280, 280], P('dp')
- new_average: float32 [192, 280, 280], P('dp')
Inputs may be any that keep to these rules, and one draw needn't show every extreme that they name: `pad_mask`: in each cell the ones come first, 512 or more of them; some cell has no zeros. `owner_map`: each block number appears once. `stat_left`: Symmetric. `stat_right`: Symmetric. `root_left`: Symmetric. `root_right`: Symmetric.
All inputs are finite; a program needn't handle non-finite values.
Results may differ from a plain program's by a relative error of at most 0.0085.
Values may be sent and summed in bfloat16 or wider, within the bound.
A program may use at most 448 MiB of HBM per device.

v0:
```python
import math
import jax
import jax.numpy as jnp
from jax import lax
from jax.sharding import PartitionSpec as P

HEADS = 20
GB = 256
PREFIX = 128
highest = lax.Precision.HIGHEST


def spread(block, axis, holder):
    block = jnp.where(lax.axis_index(axis) == holder, block, jnp.zeros_like(block))
    return lax.psum(block, axis)


def layer_norm(values, gain_row, shift_row):
    average = jnp.mean(values, axis=-1, keepdims=True)
    centred = values - average
    variance = jnp.mean(centred * centred, axis=-1, keepdims=True)
    return centred * lax.rsqrt(variance + 1e-05) * gain_row + shift_row


def gelu_tanh(values):
    return jax.nn.gelu(values, approximate=True)


def assemble(pieces, row_blocks, col_blocks):
    block_size = pieces.shape[-1]
    return (
        pieces.reshape(row_blocks, col_blocks, block_size, block_size)
        .transpose(0, 2, 1, 3)
        .reshape(row_blocks * block_size, col_blocks * block_size)
    )


def split_blocks(matrix, block_size):
    row_count, col_count = matrix.shape
    return (
        matrix.reshape(row_count // block_size, block_size, col_count // block_size, block_size)
        .transpose(0, 2, 1, 3)
        .reshape(-1, block_size, block_size)
    )


def matmul(left, right):
    return jnp.dot(left, right, preferred_element_type=jnp.float32)


def local(
    tokens,
    cotangent,
    pad_mask,
    prefix_len,
    norm_gains,
    norm_shifts,
    owner_map,
    weight_copy,
    master,
    average_weights,
    stat_left,
    stat_right,
    root_left,
    root_right,
):
    cell_count, group_len, features = tokens.shape
    row_count = cell_count * group_len
    head_size = features // HEADS
    per_group = group_len // GB
    score_scale = head_size ** (-0.5)
    slots = lax.all_gather(weight_copy, "dp", axis=0, tiled=True)
    block_count = slots.shape[0]
    block_size = slots.shape[-1]
    row_blocks = features // block_size
    col_blocks = (block_count - 4 * row_blocks * row_blocks) // (2 * row_blocks)
    square = row_blocks * row_blocks
    inverse = (
        jnp.zeros((block_count,), jnp.int32)
        .at[owner_map]
        .set(jnp.arange(block_count, dtype=jnp.int32))
    )
    blocks = jnp.take(slots, inverse, axis=0)
    w_query = assemble(blocks[0:square], row_blocks, row_blocks)
    w_key = assemble(blocks[square : 2 * square], row_blocks, row_blocks)
    w_value = assemble(blocks[2 * square : 3 * square], row_blocks, row_blocks)
    w_out = assemble(blocks[3 * square : 4 * square], row_blocks, row_blocks)
    w_up = assemble(
        blocks[4 * square : 4 * square + row_blocks * col_blocks], row_blocks, col_blocks
    )
    w_down = assemble(blocks[4 * square + row_blocks * col_blocks :], col_blocks, row_blocks)
    inputs = tokens.astype(jnp.float32).reshape(row_count, features)
    normed_one, norm_one_back = jax.vjp(layer_norm, inputs, norm_gains[0], norm_shifts[0])
    normed_in = normed_one.astype(jnp.bfloat16)
    queries = matmul(normed_in, w_query).astype(jnp.bfloat16)
    key_rows = matmul(normed_in, w_key).astype(jnp.bfloat16)
    value_rows = matmul(normed_in, w_value).astype(jnp.bfloat16)
    block_shape = (cell_count, per_group, GB, HEADS, head_size)
    query_blocks = queries.reshape(block_shape)
    key_blocks = key_rows.reshape(block_shape)
    value_blocks = value_rows.reshape(block_shape)
    key_cells = key_rows.reshape(cell_count, group_len, HEADS, head_size)
    value_cells = value_rows.reshape(cell_count, group_len, HEADS, head_size)
    prefix_keys, prefix_values = (
        spread(key_cells[:, :PREFIX], "seq", 0),
        spread(value_cells[:, :PREFIX], "seq", 0),
    )
    seq_index = lax.axis_index("seq")
    position = seq_index * group_len + jnp.arange(group_len, dtype=jnp.int32)
    alive_keys = jnp.where(
        position[None, :] < PREFIX, position[None, :] < prefix_len[:, None], pad_mask == 1
    )
    prefix_alive = jnp.arange(PREFIX, dtype=jnp.int32)[None, :] < prefix_len[:, None]
    offsets = jnp.arange(GB)
    local_seen = alive_keys.reshape(cell_count, per_group, 1, 1, GB) & (
        offsets[:, None] >= offsets[None, :]
    )
    later_block = seq_index * per_group + jnp.arange(per_group) > 0
    prefix_seen = prefix_alive[:, None, None, None, :] & later_block[None, :, None, None, None]
    visible = jnp.concatenate(
        [jnp.broadcast_to(prefix_seen, (cell_count, per_group, 1, GB, PREFIX)), local_seen], axis=-1
    )

    def score_rows():
        raw_prefix = jnp.einsum(
            "cnqhd,ckhd->cnhqk", query_blocks, prefix_keys, preferred_element_type=jnp.float32
        )
        raw_local = jnp.einsum(
            "cnqhd,cnkhd->cnhqk", query_blocks, key_blocks, preferred_element_type=jnp.float32
        )
        return jnp.where(
            visible, jnp.concatenate([raw_prefix, raw_local], axis=-1) * score_scale, -1e30
        )

    scores = score_rows()
    row_max = jnp.max(scores, axis=-1, keepdims=True)
    log_total = row_max + jnp.log(jnp.sum(jnp.exp(scores - row_max), axis=-1, keepdims=True))
    weights_low = jnp.exp(scores - log_total).astype(jnp.bfloat16)
    attended = jnp.einsum(
        "cnhqk,ckhd->cnqhd",
        weights_low[..., :PREFIX],
        prefix_values,
        preferred_element_type=jnp.float32,
    )
    attended = attended + jnp.einsum(
        "cnhqk,cnkhd->cnqhd",
        weights_low[..., PREFIX:],
        value_blocks,
        preferred_element_type=jnp.float32,
    )
    attended_low = attended.reshape(row_count, features).astype(jnp.bfloat16)
    middle = inputs + matmul(attended_low, w_out)
    normed_two, norm_two_back = jax.vjp(layer_norm, middle, norm_gains[1], norm_shifts[1])
    normed_mid = normed_two.astype(jnp.bfloat16)
    up_pre = matmul(normed_mid, w_up)
    activated, gelu_back = jax.vjp(gelu_tanh, up_pre)
    activated_low = activated.astype(jnp.bfloat16)
    block_out = (
        (middle + matmul(activated_low, w_down))
        .astype(jnp.bfloat16)
        .reshape(cell_count, group_len, features)
    )
    grad_rows = cotangent.astype(jnp.float32).reshape(row_count, features)
    grad_low = cotangent.reshape(row_count, features)
    grad_down = matmul(activated_low.T, grad_low)
    grad_act = matmul(grad_low, w_down.T)
    grad_pre = gelu_back(grad_act)[0].astype(jnp.bfloat16)
    grad_up = matmul(normed_mid.T, grad_pre)
    grad_mid_in = matmul(grad_pre, w_up.T)
    grad_middle_n, grad_gain_two, grad_shift_two = norm_two_back(grad_mid_in)
    grad_middle = grad_rows + grad_middle_n
    grad_branch = grad_middle.astype(jnp.bfloat16)
    grad_out = matmul(attended_low.T, grad_branch)
    grad_att = matmul(grad_branch, w_out.T).astype(jnp.bfloat16).reshape(block_shape)
    key_weights = jnp.exp(score_rows() - log_total)
    weights_again = key_weights.astype(jnp.bfloat16)
    grad_prob = jnp.concatenate(
        [
            jnp.einsum(
                "cnqhd,ckhd->cnhqk", grad_att, prefix_values, preferred_element_type=jnp.float32
            ),
            jnp.einsum(
                "cnqhd,cnkhd->cnhqk", grad_att, value_blocks, preferred_element_type=jnp.float32
            ),
        ],
        axis=-1,
    )
    grad_score = key_weights * (
        grad_prob - jnp.sum(key_weights * grad_prob, axis=-1, keepdims=True)
    )
    grad_raw = (grad_score * score_scale).astype(jnp.bfloat16)
    grad_raw_prefix = grad_raw[..., :PREFIX]
    grad_raw_local = grad_raw[..., PREFIX:]
    grad_query = jnp.einsum(
        "cnhqk,ckhd->cnqhd", grad_raw_prefix, prefix_keys, preferred_element_type=jnp.float32
    )
    grad_query = grad_query + jnp.einsum(
        "cnhqk,cnkhd->cnqhd", grad_raw_local, key_blocks, preferred_element_type=jnp.float32
    )
    grad_key = jnp.einsum(
        "cnhqk,cnqhd->cnkhd", grad_raw_local, query_blocks, preferred_element_type=jnp.float32
    )
    grad_value = jnp.einsum(
        "cnhqk,cnqhd->cnkhd",
        weights_again[..., PREFIX:],
        grad_att,
        preferred_element_type=jnp.float32,
    )
    grad_key_pre = jnp.einsum(
        "cnhqk,cnqhd->ckhd", grad_raw_prefix, query_blocks, preferred_element_type=jnp.float32
    )
    grad_value_pre = jnp.einsum(
        "cnhqk,cnqhd->ckhd",
        weights_again[..., :PREFIX],
        grad_att,
        preferred_element_type=jnp.float32,
    )
    summed_key, summed_value = lax.psum((grad_key_pre, grad_value_pre), "seq")
    is_owner = (seq_index == 0).astype(jnp.float32)
    grad_key = (
        grad_key.reshape(cell_count, group_len, features)
        .at[:, :PREFIX]
        .add(is_owner * summed_key.reshape(cell_count, PREFIX, features))
    )
    grad_value = (
        grad_value.reshape(cell_count, group_len, features)
        .at[:, :PREFIX]
        .add(is_owner * summed_value.reshape(cell_count, PREFIX, features))
    )
    query_grad_low = grad_query.reshape(row_count, features).astype(jnp.bfloat16)
    key_grad_low = grad_key.reshape(row_count, features).astype(jnp.bfloat16)
    value_grad_low = grad_value.reshape(row_count, features).astype(jnp.bfloat16)
    grad_wq = matmul(normed_in.T, query_grad_low)
    grad_wk = matmul(normed_in.T, key_grad_low)
    grad_wv = matmul(normed_in.T, value_grad_low)
    grad_normed = (
        matmul(query_grad_low, w_query.T)
        + matmul(key_grad_low, w_key.T)
        + matmul(value_grad_low, w_value.T)
    )
    grad_in_n, grad_gain_one, grad_shift_one = norm_one_back(grad_normed)
    grad_input = (grad_middle + grad_in_n).reshape(cell_count, group_len, features)
    grad_scale = 1.0 / math.sqrt(row_count * lax.axis_size("dp") * lax.axis_size("seq"))
    norm_terms = (
        jnp.stack([grad_gain_one, grad_shift_one, grad_gain_two, grad_shift_two]) * grad_scale
    )
    norm_grad = lax.psum(norm_terms, ("dp", "seq"))
    params = jnp.stack([norm_gains[0], norm_shifts[0], norm_gains[1], norm_shifts[1]])
    new_norms = params - 0.1 * norm_grad * lax.rsqrt(jnp.mean(norm_grad * norm_grad) + 1e-06)
    grad_blocks = (
        jnp.concatenate(
            [
                split_blocks(matrix, block_size)
                for matrix in (grad_wq, grad_wk, grad_wv, grad_out, grad_up, grad_down)
            ],
            axis=0,
        )
        * grad_scale
    )
    ordered = jnp.take(grad_blocks, owner_map, axis=0)
    owned_part = lax.psum_scatter(ordered, "dp", scatter_dimension=0, tiled=True)
    slot_grad = lax.psum(owned_part, "seq")
    new_left = (
        0.5 * stat_left
        + 0.5 * jnp.einsum("sij,skj->sik", slot_grad, slot_grad, precision=highest) / block_size
    )
    new_right = (
        0.5 * stat_right
        + 0.5 * jnp.einsum("sji,sjk->sik", slot_grad, slot_grad, precision=highest) / block_size
    )
    right_part = jnp.einsum("sij,sjk->sik", slot_grad, root_right, precision=highest)
    precond = jnp.einsum("sij,sjk->sik", root_left, right_part, precision=highest)
    new_master = master - 0.03 * precond
    new_copy = new_master.astype(jnp.bfloat16)
    new_average = 0.8 * average_weights + 0.2 * new_master
    return (
        block_out,
        grad_input,
        norm_grad,
        new_norms,
        slot_grad,
        new_left,
        new_right,
        new_master,
        new_copy,
        new_average,
    )


def solution(mesh):
    in_specs = (
        P("dp", "seq", None),
        P("dp", "seq", None),
        P("dp", "seq"),
        P("dp"),
        P(),
        P(),
        P(),
        P("dp", None, None),
        P("dp", None, None),
        P("dp", None, None),
        P("dp", None, None),
        P("dp", None, None),
        P("dp", None, None),
        P("dp", None, None),
    )
    out_specs = (
        P("dp", "seq", None),
        P("dp", "seq", None),
        P(),
        P(),
        P("dp", None, None),
        P("dp", None, None),
        P("dp", None, None),
        P("dp", None, None),
        P("dp", None, None),
        P("dp", None, None),
    )
    return jax.shard_map(local, mesh=mesh, in_specs=in_specs, out_specs=out_specs, check_vma=False)
```

profile of v0, /device:TPU:0, one launch (start us, length us, event | category | flops | bytes accessed | tf_op | source)
XLA Modules:
  0.0 2638.7 jit_solution(1818044440257464110)
XLA Ops:
  16.7 420.8 %all-gather.2.cloned.1.call-done = bf16[192,280,280]{2,1,0:T(8,128)(2,1)} async-done(((bf16[12,280,280]{2,1,0:T(8,128)(2,1)}), bf16[192,280,280]{2,1,0:T(8,128)(2,1)}) %all-gather.2.cloned.1.call-update) | async-done | bytes 30105616 | tf_op jit(solution)/shard_map/all_gather | solution.py:72
  437.5 28.3 %gather_fusion = bf16[192,280,280]{2,1,0:T(8,128)(2,1)} fusion(bf16[192,280,280]{2,1,0:T(8,128)(2,1)} %all-gather.2.cloned.1.call-done, s32[1024]{0:T(1024)S(1)} %pad_clamp_fusion.1), kind=kCustom, calls=%fused_computation | custom fusion | bytes 60211968 | tf_op jit(solution)/shard_map/jit(_take)/gather | solution.py:83
  465.8 28.1 %broadcast_select_fusion.1 = bf16[192,280,280]{2,1,0:T(8,128)(2,1)} fusion(bf16[192,280,280]{2,1,0:T(8,128)(2,1)} %gather_fusion, pred[192]{0:T(512)(128)(4,1)S(1)} %compare_and_fusion.1), kind=kLoop, calls=%fused_computation.5 | loop fusion | flops 15052800 | bytes 60211392 | tf_op jit(solution)/shard_map/jit(_take)/select_n | solution.py:83
  493.9 9.3 fusion.111
  503.2 21.0 fusion.110
  527.4 6.3 reshape.760
  538.7 6.3 reshape.764
  545.0 6.7 convolution_convert_fusion.3
  551.7 5.1 convolution_convert_fusion.2
  559.9 6.3 reshape.768
  569.7 6.6 convolution_convert_fusion.1
  576.3 5.6 reshape.772
  589.3 5.9 copy.248
  595.2 6.3 reshape.775
  601.5 22.4 copy.115
  623.9 21.1 reshape.779
  644.9 14.3 copy.247
  659.3 21.4 reshape.777
  680.7 11.6 convolution_bitcast_fusion.1
  695.0 13.9 fusion.108
  709.7 6.5 exponential_reduce_fusion
  716.3 9.9 fusion.1
  726.2 5.2 fusion.22
  741.5 26.2 fusion.16
  767.8 31.0 %fusion.8 = bf16[1024,4480]{1,0:T(8,128)(2,1)} fusion(f32[1024,4480]{1,0:T(8,128)} %get-tuple-element.100, bf16[4480,1120]{0,1:T(8,128)(2,1)} %reshape.779, bf16[1,1024,1120]{1,2,0:T(8,128)(2,1)S(1)} %copy-done.12), kind=kOutput, calls=%fused_computation.23 | convolution fusion | flops 10367795200 | bytes 39854080 | tf_op jit(solution)/shard_map/dot_general | solution.py:48
  798.8 19.8 multiply_reduce_fusion.1
  832.3 9.6 convolution_bitcast_fusion.4
  842.0 8.6 convolution_bitcast_fusion
  850.6 5.4 convolution_bitcast_fusion.2
  856.0 5.2 fusion.74
  861.1 20.7 multiply_reduce_fusion
  881.8 22.1 multiply_convert_fusion
  903.9 5.5 copy-done.1
  912.1 8.7 fusion.20
  920.8 9.6 convolution_bitcast_fusion.5
  930.5 18.1 fusion.103
  948.6 5.1 copy.134
  953.7 6.5 reshape.790
  977.7 6.5 reshape.787
  988.5 28.5 %reshape.801 = f32[4,280,16,280]{3,2,1,0:T(8,128)} reshape(f32[1120,4480]{1,0:T(8,128)} %fusion.103) | data formatting | bytes 40140800 | tf_op jit(solution)/shard_map/reshape | solution.py:41
  1017.1 27.0 %copy.138 = f32[4,280,16,280]{3,1,2,0:T(8,128)} copy(f32[4,280,16,280]{3,2,1,0:T(8,128)} %reshape.801) | data formatting | bytes 40140800 | tf_op jit(solution)/shard_map/reshape | solution.py:41
  1044.0 12.7 copy.139
  1056.8 20.0 fusion.117
  1081.6 5.8 fusion.116
  1091.6 5.7 fusion.120
  1121.3 7.6 fusion.115
  1132.6 6.8 constant_dynamic-update-slice_fusion.3
  1139.4 6.4 constant_dynamic-update-slice_fusion.2
  1145.9 9.4 constant_dynamic-update-slice_fusion.1
  1155.3 20.5 constant_dynamic-update-slice_fusion
  1175.8 55.9 %broadcast_multiply_fusion = f32[192,280,280]{2,1,0:T(8,128)} fusion(f32[192,280,280]{2,1,0:T(8,128)} %constant_dynamic-update-slice_fusion), kind=kLoop, calls=%fused_computation.4 | loop fusion | flops 15052800 | bytes 120422400 | tf_op jit(solution)/shard_map/mul | solution.py:251
  1231.7 56.4 %gather_fusion.1 = f32[192,280,280]{2,1,0:T(8,128)} fusion(f32[192,280,280]{2,1,0:T(8,128)} %broadcast_multiply_fusion, s32[1024]{0:T(1024)} %pad_clamp_fusion), kind=kCustom, calls=%fused_computation.1 | custom fusion | bytes 120423168 | tf_op jit(solution)/shard_map/jit(_take)/gather | solution.py:260
  1288.1 54.1 %broadcast_select_fusion = f32[192,280,280]{2,1,0:T(8,128)} fusion(f32[192,280,280]{2,1,0:T(8,128)} %gather_fusion.1, pred[192]{0:T(512)(128)(4,1)S(1)} %copy-done.57), kind=kLoop, calls=%fused_computation.3 | loop fusion | flops 15052800 | bytes 120422592 | tf_op jit(solution)/shard_map/jit(_take)/select_n | solution.py:260
  1342.2 1134.6 %reduce-scatter.2.cloned.1.call-done = f32[12,280,280]{2,1,0:T(8,128)} async-done(((f32[192,280,280]{2,1,0:T(8,128)}), f32[12,280,280]{2,1,0:T(8,128)}) %reduce-scatter.2.cloned.1.call-update) | async-done | bytes 3763216 | tf_op jit(solution)/shard_map/reduce_scatter | solution.py:261
  2476.8 6.1 copy.143
  2483.0 6.5 copy.142
  2489.6 19.8 fusion.54
  2509.4 39.9 %psum.46 = f32[4,1120]{1,0:T(4,128)S(1)} all-reduce(f32[4,1120]{1,0:T(4,128)S(1)} %maximum_multiply_fusion.1), channel_id=1, replica_groups=mesh['dp'=16,'seq'=2] {'dp','seq'}, use_global_device_ids=true, to_apply=%region_20.21 | all-reduce | flops 4480 | bytes 35840 | tf_op jit(solution)/shard_map/psum | solution.py:247
  2551.3 14.1 fusion.118
  2565.4 17.3 multiply_add_fusion
  2582.7 6.1 copy.144
  2591.6 6.2 copy.146
  2597.8 16.9 multiply_add_fusion.2
  2614.7 14.9 multiply_add_fusion.1
  (258 shorter events, 125.6 us)
Async XLA Ops:
  7.2 6.6 copy-start.5
  7.2 8.3 copy-start.51
  7.2 8.2 copy-start.52
  7.2 430.3 %all-gather.2.cloned.1.call-start = ((), (), s32[]{:S(2)}) async-start(), calls=%async_computation.1 | async-start | bytes 43868160 | tf_op jit(solution)/shard_map/all_gather | solution.py:72
  7.9 684.3 %all-reduce.10.cloned.1.call-start = ((), (), s32[]{:S(2)}) async-start(), calls=%async_computation.5 | async-start | bytes 1146880 | tf_op jit(solution)/shard_map/psum | solution.py:15
  14.2 555.5 %copy-start.34 = (f32[1024]{0:T(1024)}, f32[1024]{0:T(1024)S(1)}, u32[]{:S(2)}) copy-start(f32[1024]{0:T(1024)S(1)} %broadcast_multiply_fusion.4) | copy-start | bytes 12292
  15.5 554.3 %copy-start.40 = (f32[1024]{0:T(1024)}, f32[1024]{0:T(1024)S(1)}, u32[]{:S(2)}) copy-start(f32[1024]{0:T(1024)S(1)} %fusion.95) | copy-start | bytes 12292
  16.7 553.0 %copy-start.32 = (f32[1120]{0:T(1024)}, f32[1120]{0:T(1024)S(1)}, u32[]{:S(2)}) copy-start(f32[1120]{0:T(1024)S(1)} %get-tuple-element.104) | copy-start | bytes 13444
  16.7 553.0 %copy-start.42 = (f32[1120]{0:T(1024)}, f32[1120]{0:T(1024)S(1)}, u32[]{:S(2)}) copy-start(f32[1120]{0:T(1024)S(1)} %get-tuple-element.73) | copy-start | bytes 13444
  545.0 6.7 copy-start.16
  569.7 517.7 %all-reduce.8.cloned.1.call-start = ((), (), s32[]{:S(2)}) async-start(), calls=%async_computation.4 | async-start | bytes 2293760 | tf_op jit(solution)/shard_map/psum | solution.py:218
  589.3 103.0 %copy-start.2 = (bf16[4,256,20,56]{1,0,3,2:T(4,128)(2,1)}, bf16[4,256,20,56]{1,0,3,2:T(4,128)(2,1)S(1)}, u32[]{:S(2)}) copy-start(bf16[4,256,20,56]{1,0,3,2:T(4,128)(2,1)S(1)} %reshape.769) | copy-start | bytes 6881284
  692.3 16.6 slice-start
  692.3 16.6 slice-start.1
  695.0 21.3 copy-start
  695.0 14.0 slice-start.2
  695.0 14.0 slice-start.3
  695.0 14.7 slice-start.4
  716.3 9.9 copy-start.10
  740.9 77.7 %copy-start.8 = (f32[1024,1120]{0,1:T(8,128)}, f32[1024,1120]{0,1:T(8,128)S(1)}, u32[]{:S(2)}) copy-start(f32[1024,1120]{0,1:T(8,128)S(1)} %get-tuple-element.95) | copy-start | bytes 13762564
  741.5 26.3 copy-start.12
  832.3 9.6 copy-start.11
  881.8 27.6 %copy-start.3 = (bf16[4,256,20,56]{1,0,3,2:T(4,128)(2,1)S(1)}, bf16[4,256,20,56]{1,0,3,2:T(4,128)(2,1)}, u32[]{:S(2)}) copy-start(bf16[4,256,20,56]{1,0,3,2:T(4,128)(2,1)} %copy-done.2) | copy-start | bytes 6881284
  912.1 18.3 slice-start.16
  920.8 9.6 slice-start.17
  920.8 9.6 copy-start.54
  920.8 27.8 %slice-start.18 = ((s8[4587520]{0:T(1024)(128)(4,1)}), s8[4194304]{0:T(1024)(128)(4,1)S(1)}, s32[]{:S(2)}) async-start(s8[4587520]{0:T(1024)(128)(4,1)} %bitcast.354), calls=%async_computation.24 | async-start | bytes 8388608
  930.4 18.1 slice-start.19
  960.2 12.5 slice-start.20
  964.7 8.0 slice-start.21
  1044.0 12.7 copy-start.13
  1056.7 1420.1 %reduce-scatter.2.cloned.1.call-start = ((), (), s32[]{:S(2)}) async-start(), calls=%async_computation.2 | async-start | bytes 87736320 | tf_op jit(solution)/shard_map/reduce_scatter | solution.py:261
  1056.8 20.0 copy-start.17
  1056.8 20.0 copy-start.22
  1089.6 9.2 slice-start.22
  1091.6 5.8 copy-start.24
  1091.6 7.2 copy-start.7
  1091.6 7.2 copy-start.15
  1091.6 7.2 copy-start.33
  1091.6 7.2 copy-start.35
  1091.6 7.2 slice-start.23
  1097.4 8.6 slice-start.14
  1098.9 7.1 slice-start.15
  1110.3 7.1 copy-start.28
  1121.3 24.5 slice-start.7
  1121.3 24.5 slice-start.8
  1121.3 24.5 slice-start.9
  1128.9 16.9 slice-start.10
  1132.6 13.2 slice-start.11
  1132.6 13.2 slice-start.12
  1139.4 6.4 slice-start.13
  1231.7 56.4 %copy-start.57 = (pred[192]{0:T(512)(128)(4,1)S(1)}, pred[192]{0:T(512)(128)(4,1)}, u32[]{:S(2)}) copy-start(pred[192]{0:T(512)(128)(4,1)} %compare_and_fusion) | copy-start | bytes 580
  1342.2 1209.1 %all-reduce.6.cloned.1.call-start = ((), (), s32[]{:S(2)}) async-start(), calls=%async_computation.3 | async-start | bytes 10321920 | tf_op jit(solution)/shard_map/psum | solution.py:262
  2483.0 6.5 copy-start.56
  2483.0 6.5 copy-start.55
  2489.5 19.9 copy-start.46
  2489.5 19.9 copy-start.45
  2489.5 61.1 %copy-start.47 = (f32[1,1120]{1,0:T(1,128)S(1)}, f32[1,1120]{1,0:T(1,128)}, u32[]{:S(2)}) copy-start(f32[1,1120]{1,0:T(1,128)} %get-tuple-element.91) | copy-start | bytes 13444
  2489.5 61.1 %copy-start.48 = (f32[1,1120]{1,0:T(1,128)S(1)}, f32[1,1120]{1,0:T(1,128)}, u32[]{:S(2)}) copy-start(f32[1,1120]{1,0:T(1,128)} %get-tuple-element.93) | copy-start | bytes 13444
  2489.5 61.1 %copy-start.49 = (f32[1,1120]{1,0:T(1,128)S(1)}, f32[1,1120]{1,0:T(1,128)}, u32[]{:S(2)}) copy-start(f32[1,1120]{1,0:T(1,128)} %get-tuple-element.102) | copy-start | bytes 13444
  2489.6 61.1 %copy-start.50 = (f32[1,1120]{1,0:T(1,128)S(1)}, f32[1,1120]{1,0:T(1,128)}, u32[]{:S(2)}) copy-start(f32[1,1120]{1,0:T(1,128)} %get-tuple-element.103) | copy-start | bytes 13444
  2549.3 16.1 copy-start.31
  2591.6 23.1 slice-start.5
  2597.8 16.9 slice-start.6
  (23 other events, 84.3 us)
Sparse Core Ops, SparseCore 0:
  10.8 426.5 all-gather.1
  569.8 17.0 all-reduce.9
  1056.8 18.0 all-reduce.7
  1342.3 1134.4 reduce-scatter.1
  2479.3 29.0 all-reduce.5
where the time goes:
time: 2650 us; the launch traced here: 2640 us
  waiting for transfers between devices  1560 us (59%)
  local copies, waits for them, and re-layouts  452 us (17%)
  matrix products  338 us (13%)
  other arithmetic  236 us (9%)
  blocking collectives  39.9 us (2%)
    reduce_scatter x1, waiting for transfers between devices, local(): lax.psum_scatter(ordered, 'dp', scatter_dimension=0, tiled=True)  1130 us
    all_gather x1, waiting for transfers between devices, local(): slots = lax.all_gather(weight_copy, 'dp', axis=0, tiled=True)  421 us
    dot_general x18, matrix products, matmul(): return jnp.dot(left, right, preferred_element_type=jnp.float32)  197 us
    unnamed x179, local copies, waits for them, and re-layouts  81.6 us
    reshape x6, local copies, waits for them, and re-layouts, assemble(): return pieces.reshape(row_blocks, col_blocks, block_size, block_size).tra...  67.7 us
    gather x1, local copies, waits for them, and re-layouts, local(): ordered = jnp.take(grad_blocks, owner_map, axis=0)  56.4 us
    mul x1, other arithmetic, local(): jnp.concatenate([split_blocks(matrix, block_size) for matrix in (grad_wq,...  55.9 us
    reshape x2, local copies, waits for them, and re-layouts, split_blocks(): matrix.reshape(row_count // block_size, block_size, col_count // block_si...  55.5 us
  transfers between devices with their start and end apart: 5, of which 2 were waited for; matrix products, arithmetic and copies ran while one was open for 7% of the time, Pallas kernels for 0%

commit v1 on v0

--- a/solution.py
+++ b/solution.py
@@ -69,7 +69,14 @@
     head_size = features // HEADS
     per_group = group_len // GB
     score_scale = head_size ** (-0.5)
-    slots = lax.all_gather(weight_copy, "dp", axis=0, tiled=True)
+    ways, here, lap = (lax.axis_size("dp"), lax.axis_index("dp"), weight_copy.shape[0])
+    line, have = (weight_copy, 1)
+    while have < ways:
+        line = jnp.concatenate(
+            [line, lax.ppermute(line, "dp", [(d, (d - have) % ways) for d in range(ways)])], axis=0
+        )
+        have = 2 * have
+    slots = jnp.roll(line, here * lap, axis=0)
     block_count = slots.shape[0]
     block_size = slots.shape[-1]
     row_blocks = features // block_size

time: 2650 us -> 3650 us (1.38)
  waiting for transfers between devices: 1560 us -> 2370 us
  local copies, waits for them, and re-layouts: 452 us -> 607 us
    ppermute x0 -> x4, waiting for transfers between devices: none -> 1230 us  [local(): lax.ppermute(line, 'dp', [(d, (d - have) % ways) for d in range(ways)])]
    all_gather x1 -> x0, waiting for transfers between devices: 421 us -> none  [local(): slots = lax.all_gather(weight_copy, 'dp', axis=0, tiled=True)]
    reshape x6 -> x0, local copies, waits for them, and re-layouts: 53.9 us -> none  [assemble(): pieces.reshape(row_blocks, col_blocks, block_size, block_size)]
    transpose x0 -> x6, local copies, waits for them, and re-layouts: none -> 52.4 us  [assemble(): return pieces.reshape(row_blocks, col_blocks, block_size, block_size).tra...]
    unnamed x179 -> x218, local copies, waits for them, and re-layouts: 81.6 us -> 134 us
    concatenate x0 -> x2, local copies, waits for them, and re-layouts: none -> 47.9 us  [the longest x1 30.5 us: local(): jnp.concatenate([line, lax.ppermute(line, 'dp', [(d, (d - have) % ways) f...]
  transfers between devices with their start and end apart: 5 -> 8, of which waited for: 2 -> 5; matrix products, arithmetic and copies ran while one was open for 7% -> 6% of each run, Pallas kernels for 0% -> 0%
where the time goes in v1:
time: 3650 us; the launch traced here: 3630 us
  waiting for transfers between devices  2370 us (65%)
  local copies, waits for them, and re-layouts  607 us (17%)
  matrix products  338 us (9%)
  other arithmetic  257 us (7%)
  blocking collectives  39.8 us (1%)
    ppermute x4, waiting for transfers between devices, local(): lax.ppermute(line, 'dp', [(d, (d - have) % ways) for d in range(ways)])  1230 us
    reduce_scatter x1, waiting for transfers between devices, local(): lax.psum_scatter(ordered, 'dp', scatter_dimension=0, tiled=True)  1140 us
    dot_general x18, matrix products, matmul(): return jnp.dot(left, right, preferred_element_type=jnp.float32)  197 us
    unnamed x218, local copies, waits for them, and re-layouts  134 us
  transfers between devices with their start and end apart: 8, of which 5 were waited for; matrix products, arithmetic and copies ran while one was open for 6% of the time, Pallas kernels for 0%

profile of v1, /device:TPU:0, one launch (start us, length us, event | category | flops | bytes accessed | tf_op | source)
XLA Modules:
  0.0 3634.4 jit_solution(9172140450231348548)
XLA Ops:
  7.2 7.0 collective-permute-start
  14.2 55.6 %collective-permute-done = bf16[12,280,280]{2,1,0:T(8,128)(2,1)S(1)} collective-permute-done((bf16[12,280,280]{2,1,0:T(8,128)(2,1)}, bf16[12,280,280]{2,1,0:T(8,128)(2,1)S(1)}, u32[]{:S(2)}, u32[]{:S(2)}) %collective-permute-start) | collective-permute-done | bytes 1881632 | tf_op jit(solution)/shard_map/ppermute | solution.py:76
  74.8 110.7 %collective-permute-done.1 = bf16[24,280,280]{2,1,0:T(8,128)(2,1)S(1)} collective-permute-done((bf16[24,280,280]{2,1,0:T(8,128)(2,1)S(1)}, bf16[24,280,280]{2,1,0:T(8,128)(2,1)S(1)}, u32[]{:S(2)}, u32[]{:S(2)}) %collective-permute-start.1) | collective-permute-done | bytes 3763232 | tf_op jit(solution)/shard_map/ppermute | solution.py:76
  188.1 221.3 %collective-permute-done.2 = bf16[48,280,280]{2,1,0:T(8,128)(2,1)S(1)} collective-permute-done((bf16[48,280,280]{2,1,0:T(8,128)(2,1)S(1)}, bf16[48,280,280]{2,1,0:T(8,128)(2,1)S(1)}, u32[]{:S(2)}, u32[]{:S(2)}) %collective-permute-start.2) | collective-permute-done | bytes 7526432 | tf_op jit(solution)/shard_map/ppermute | solution.py:76
  413.3 15.1 pad_maximum_fusion.1
  428.4 30.5 copy.153
  472.7 8.8 constant_dynamic-update-slice_fusion.6
  481.5 838.1 %collective-permute-done.3 = bf16[96,280,280]{0,2,1:T(8,128)(2,1)} collective-permute-done((bf16[96,280,280]{0,2,1:T(8,128)(2,1)}, bf16[96,280,280]{0,2,1:T(8,128)(2,1)}, u32[]{:S(2)}, u32[]{:S(2)}) %collective-permute-start.3) | collective-permute-done | bytes 15052832 | tf_op jit(solution)/shard_map/ppermute | solution.py:76
  1319.7 31.6 copy.154
  1351.3 17.7 constant_dynamic-update-slice_fusion.5
  1376.1 8.7 constant_dynamic-update-slice_fusion.1
  1384.9 17.4 constant_dynamic-update-slice_fusion
  1402.3 28.0 constant_dynamic-slice_fusion
  1430.3 28.1 gather_fusion
  1458.4 28.2 broadcast_select_fusion.1
  1486.6 9.3 fusion.111
  1496.0 21.0 fusion.110
  1527.3 6.3 reshape.764
  1533.7 6.9 convolution_convert_fusion.3
  1548.6 6.3 reshape.768
  1558.4 6.8 convolution_convert_fusion.1
  1584.1 6.3 reshape.775
  1590.4 22.5 copy.170
  1612.9 21.1 reshape.779
  1634.0 14.3 copy.169
  1648.3 21.5 reshape.777
  1669.8 11.6 convolution_bitcast_fusion.1
  1684.1 13.9 fusion.108
  1698.9 6.5 exponential_reduce_fusion
  1705.5 9.9 fusion.1
  1730.7 26.3 fusion.16
  1756.9 30.9 fusion.8
  1787.9 19.8 multiply_reduce_fusion.1
  1821.4 9.6 convolution_bitcast_fusion.4
  1831.0 8.6 convolution_bitcast_fusion
  1850.2 20.7 multiply_reduce_fusion
  1870.9 22.1 multiply_convert_fusion
  1901.2 8.7 fusion.20
  1909.9 9.6 convolution_bitcast_fusion.5
  1919.5 18.5 fusion.103
  1943.1 6.5 reshape.790
  1967.1 6.5 reshape.787
  1977.9 28.5 reshape.801
  2006.4 27.0 copy.193
  2033.4 12.7 copy.194
  2046.2 19.9 fusion.117
  2110.6 7.6 fusion.115
  2121.9 6.8 constant_dynamic-update-slice_fusion.13
  2128.6 6.4 constant_dynamic-update-slice_fusion.12
  2135.1 9.4 constant_dynamic-update-slice_fusion.11
  2144.5 20.7 constant_dynamic-update-slice_fusion.10
  2165.1 56.0 %broadcast_multiply_fusion = f32[192,280,280]{2,1,0:T(8,128)} fusion(f32[192,280,280]{2,1,0:T(8,128)} %constant_dynamic-update-slice_fusion.10), kind=kLoop, calls=%fused_computation.4 | loop fusion | flops 15052800 | bytes 120422400 | tf_op jit(solution)/shard_map/mul | solution.py:258
  2221.2 56.3 %gather_fusion.1 = f32[192,280,280]{2,1,0:T(8,128)} fusion(f32[192,280,280]{2,1,0:T(8,128)} %broadcast_multiply_fusion, s32[1024]{0:T(1024)} %pad_clamp_fusion), kind=kCustom, calls=%fused_computation.1 | custom fusion | bytes 120423168 | tf_op jit(solution)/shard_map/jit(_take)/gather | solution.py:267
  2277.5 54.2 %broadcast_select_fusion = f32[192,280,280]{2,1,0:T(8,128)} fusion(f32[192,280,280]{2,1,0:T(8,128)} %gather_fusion.1, pred[192]{0:T(512)(128)(4,1)S(1)} %copy-done.68), kind=kLoop, calls=%fused_computation.3 | loop fusion | flops 15052800 | bytes 120422592 | tf_op jit(solution)/shard_map/jit(_take)/select_n | solution.py:267
  2331.7 1140.8 %reduce-scatter.2.cloned.1.call-done = f32[12,280,280]{2,1,0:T(8,128)} async-done(((f32[192,280,280]{2,1,0:T(8,128)}), f32[12,280,280]{2,1,0:T(8,128)}) %reduce-scatter.2.cloned.1.call-update) | async-done | bytes 3763216 | tf_op jit(solution)/shard_map/reduce_scatter | solution.py:268
  3472.5 6.1 copy.198
  3478.6 6.6 copy.197
  3485.3 19.8 fusion.54
  3505.2 39.8 %psum.46 = f32[4,1120]{1,0:T(4,128)S(1)} all-reduce(f32[4,1120]{1,0:T(4,128)S(1)} %maximum_multiply_fusion.1), channel_id=1, replica_groups=mesh['dp'=16,'seq'=2] {'dp','seq'}, use_global_device_ids=true, to_apply=%region_20.21 | all-reduce | flops 4480 | bytes 35840 | tf_op jit(solution)/shard_map/psum | solution.py:254
  3547.0 14.1 fusion.118
  3561.1 17.3 multiply_add_fusion
  3587.3 6.2 copy.201
  3593.5 17.0 multiply_add_fusion.2
  3610.4 14.9 multiply_add_fusion.1
  (310 shorter events, 211.0 us)
Async XLA Ops:
  7.2 178.4 %copy-start.4 = (bf16[12,280,280]{2,1,0:T(8,128)(2,1)S(1)}, bf16[12,280,280]{2,1,0:T(8,128)(2,1)}, u32[]{:S(2)}) copy-start(bf16[12,280,280]{2,1,0:T(8,128)(2,1)} %param.25) | copy-start | bytes 5644804
  7.2 1674.2 %all-reduce.10.cloned.1.call-start = ((), (), s32[]{:S(2)}) async-start(), calls=%async_computation.4 | async-start | bytes 1146880 | tf_op jit(solution)/shard_map/psum | solution.py:15
  7.2 62.5 %collective-permute-start = (bf16[12,280,280]{2,1,0:T(8,128)(2,1)}, bf16[12,280,280]{2,1,0:T(8,128)(2,1)S(1)}, u32[]{:S(2)}, u32[]{:S(2)}) collective-permute-start(bf16[12,280,280]{2,1,0:T(8,128)(2,1)} %param.25), channel_id=1, source_target_pairs={{0,30},{2,0},{4,2},{6,4},{8,6},{10,8},{12,10},{14,12},{16,14},{18,... | collective-permute-start | bytes 5644808 | tf_op jit(solution)/shard_map/ppermute | solution.py:76
  69.8 339.7 %copy-start.5 = (bf16[12,280,280]{2,1,0:T(8,128)(2,1)}, bf16[12,280,280]{2,1,0:T(8,128)(2,1)S(1)}, u32[]{:S(2)}) copy-start(bf16[12,280,280]{2,1,0:T(8,128)(2,1)S(1)} %collective-permute-done) | copy-start | bytes 5644804
  73.3 112.2 %collective-permute-start.1 = (bf16[24,280,280]{2,1,0:T(8,128)(2,1)S(1)}, bf16[24,280,280]{2,1,0:T(8,128)(2,1)S(1)}, u32[]{:S(2)}, u32[]{:S(2)}) collective-permute-start(bf16[24,280,280]{2,1,0:T(8,128)(2,1)S(1)} %pad_maximum_fusion.3), channel_id=1, source_target_pairs={{0,28},{2,30},{4,0},{6,2},{8,4},{10,6},{12,8},{14,10},{16,12},{18,... | collective-permute-start | bytes 11289608 | tf_op jit(solution)/shard_map/ppermute | solution.py:76
  185.5 223.9 %copy-start.3 = (bf16[24,280,280]{2,1,0:T(8,128)(2,1)}, bf16[24,280,280]{2,1,0:T(8,128)(2,1)S(1)}, u32[]{:S(2)}) copy-start(bf16[24,280,280]{2,1,0:T(8,128)(2,1)S(1)} %collective-permute-done.1) | copy-start | bytes 11289604
  187.6 221.9 %collective-permute-start.2 = (bf16[48,280,280]{2,1,0:T(8,128)(2,1)S(1)}, bf16[48,280,280]{2,1,0:T(8,128)(2,1)S(1)}, u32[]{:S(2)}, u32[]{:S(2)}) collective-permute-start(bf16[48,280,280]{2,1,0:T(8,128)(2,1)S(1)} %pad_maximum_fusion.2), channel_id=1, source_target_pairs={{0,24},{2,26},{4,28},{6,30},{8,0},{10,2},{12,4},{14,6},{16,8},{18,... | collective-permute-start | bytes 22579208 | tf_op jit(solution)/shard_map/ppermute | solution.py:76
  428.4 31.2 copy-start.67
  428.4 31.2 copy-start.66
  458.9 860.8 %collective-permute-start.3 = (bf16[96,280,280]{0,2,1:T(8,128)(2,1)}, bf16[96,280,280]{0,2,1:T(8,128)(2,1)}, u32[]{:S(2)}, u32[]{:S(2)}) collective-permute-start(bf16[96,280,280]{0,2,1:T(8,128)(2,1)} %copy.153), channel_id=1, source_target_pairs={{0,16},{2,18},{4,20},{6,22},{8,24},{10,26},{12,28},{14,30},{16,0},... | collective-permute-start | bytes 45158408 | tf_op jit(solution)/shard_map/ppermute | solution.py:76
  462.0 7.9 slice-start.14
  1319.7 53.7 %slice-start.16 = ((s8[5160960]{0:T(1024)(128)(4,1)}), s8[966656]{0:T(1024)(128)(4,1)S(1)}, s32[]{:S(2)}) async-start(s8[5160960]{0:T(1024)(128)(4,1)} %bitcast.341), calls=%async_computation.21 | async-start | bytes 1933312
  1351.3 22.2 slice-start.17
  1522.1 11.6 copy-start.12
  1522.1 11.6 copy-start.40
  1522.1 11.6 copy-start.43
  1522.1 11.6 copy-start.49
  1522.1 11.6 copy-start.51
  1558.3 518.3 %all-reduce.8.cloned.1.call-start = ((), (), s32[]{:S(2)}) async-start(), calls=%async_computation.3 | async-start | bytes 2293760 | tf_op jit(solution)/shard_map/psum | solution.py:225
  1578.1 103.2 %copy-start.8 = (bf16[4,256,20,56]{1,0,3,2:T(4,128)(2,1)}, bf16[4,256,20,56]{1,0,3,2:T(4,128)(2,1)S(1)}, u32[]{:S(2)}) copy-start(bf16[4,256,20,56]{1,0,3,2:T(4,128)(2,1)S(1)} %reshape.769) | copy-start | bytes 6881284
  1681.4 16.6 slice-start
  1681.4 16.6 slice-start.1
  1684.1 21.4 copy-start
  1684.1 14.0 slice-start.2
  1684.1 14.0 slice-start.3
  1684.1 14.7 slice-start.4
  1705.5 9.9 copy-start.18
  1730.1 77.6 %copy-start.15 = (f32[1024,1120]{0,1:T(8,128)}, f32[1024,1120]{0,1:T(8,128)S(1)}, u32[]{:S(2)}) copy-start(f32[1024,1120]{0,1:T(8,128)S(1)} %get-tuple-element.105) | copy-start | bytes 13762564
  1730.7 26.3 copy-start.20
  1821.4 9.6 copy-start.19
  1870.9 27.6 copy-start.9
  1901.2 18.3 slice-start.20
  1909.8 9.6 slice-start.21
  1909.9 9.6 copy-start.63
  1909.9 28.1 slice-start.22
  1919.5 18.5 slice-start.23
  1949.6 12.4 slice-start.24
  1954.1 7.9 slice-start.25
  2033.4 12.7 copy-start.21
  2046.1 1426.3 %reduce-scatter.2.cloned.1.call-start = ((), (), s32[]{:S(2)}) async-start(), calls=%async_computation.1 | async-start | bytes 87736320 | tf_op jit(solution)/shard_map/reduce_scatter | solution.py:268
  2046.2 20.0 copy-start.25
  2046.2 19.9 copy-start.30
  2078.8 9.2 slice-start.26
  2080.9 7.2 copy-start.41
  2080.9 7.2 copy-start.44
  2080.9 7.2 slice-start.27
  2086.6 8.6 slice-start.18
  2110.5 24.5 slice-start.7
  2110.5 24.5 slice-start.8
  2110.6 24.5 slice-start.9
  2118.1 16.9 slice-start.10
  2121.8 13.2 slice-start.11
  2121.8 13.2 slice-start.12
  2221.2 56.3 %copy-start.68 = (pred[192]{0:T(512)(128)(4,1)S(1)}, pred[192]{0:T(512)(128)(4,1)}, u32[]{:S(2)}) copy-start(pred[192]{0:T(512)(128)(4,1)} %get-tuple-element.116) | copy-start | bytes 580
  2331.7 1215.3 %all-reduce.6.cloned.1.call-start = ((), (), s32[]{:S(2)}) async-start(), calls=%async_computation.2 | async-start | bytes 10321920 | tf_op jit(solution)/shard_map/psum | solution.py:269
  3485.2 19.9 copy-start.55
  3485.2 19.9 copy-start.54
  3485.3 61.1 %copy-start.56 = (f32[1,1120]{1,0:T(1,128)S(1)}, f32[1,1120]{1,0:T(1,128)}, u32[]{:S(2)}) copy-start(f32[1,1120]{1,0:T(1,128)} %get-tuple-element.101) | copy-start | bytes 13444
  3485.3 61.1 %copy-start.57 = (f32[1,1120]{1,0:T(1,128)S(1)}, f32[1,1120]{1,0:T(1,128)}, u32[]{:S(2)}) copy-start(f32[1,1120]{1,0:T(1,128)} %get-tuple-element.103) | copy-start | bytes 13444
  3485.3 61.1 %copy-start.58 = (f32[1,1120]{1,0:T(1,128)S(1)}, f32[1,1120]{1,0:T(1,128)}, u32[]{:S(2)}) copy-start(f32[1,1120]{1,0:T(1,128)} %get-tuple-element.112) | copy-start | bytes 13444
  3485.3 61.1 %copy-start.59 = (f32[1,1120]{1,0:T(1,128)S(1)}, f32[1,1120]{1,0:T(1,128)}, u32[]{:S(2)}) copy-start(f32[1,1120]{1,0:T(1,128)} %get-tuple-element.113) | copy-start | bytes 13444
  3545.0 16.1 copy-start.39
  3587.3 23.2 slice-start.5
  3593.5 17.0 slice-start.6
  (41 other events, 179.6 us)
Sparse Core Ops, SparseCore 0:
  1558.4 23.6 all-reduce.9
  2046.3 24.5 all-reduce.7
  2331.8 1140.6 reduce-scatter.1
  3475.0 28.9 all-reduce.5
